TPU v7x, 128 devices: a whole 4x4x4 slice. The times are simulated.
128 devices in a mesh: slab: 16 (over y, x), grp: 8 (over z, core).
Axes of the slice: x: 4, y: 4, z: 4, core: 2. Of those that a mesh axis runs over, the one named last changes fastest.
Arguments:
- initial: float32 [32, 64, 32, 256], P('grp', 'slab'), may hold values from 0 to 1
- target: float32 [32, 64, 32, 256], P('grp', 'slab'), may hold values from 0 to 0.6
- birth_step: int32 [64, 32, 256], P('slab'), may hold values from 0 to 4, as said below
- classes: int32 [32], P('grp'), may hold values from 0 to 3
- mobility: float32 [4, 4], replicated, may hold values from 0.2 to 2
Outputs:
- final_state: float32 [32, 64, 32, 256], P('grp', 'slab')
- initial_grad: float32 [32, 64, 32, 256], P('grp', 'slab')
- mobility_grad: float32 [4, 4], replicated
Inputs may be any that keep to these rules, and one draw needn't show every extreme that they name: A voxel takes part in step n when birth_step <= n; the value 4 means that it never takes part in the window; exactly one voxel has the value 0.
All inputs are finite; a program needn't handle non-finite values.
Results may differ from a plain program's by a relative error of at most 0.0001.
Values sent between devices are 32-bit elements; how exact they have to be, the bound alone decides.
No kernel may reach another device: no remote copies, remote signals or barrier semaphores. Data moves between devices by JAX's collectives and lax.ppermute only.
A program may use at most 64 MiB of HBM per device.

v0:
```python
import jax
import jax.numpy as jnp
from jax import lax
from jax.sharding import PartitionSpec as P

STEPS = 4
coupling = 0.3
stiffness = 1.0
time_step = 0.06


def extended_2(cells, sides, width):
    for axis, dim in sides:
        count = lax.axis_size(axis)
        ends = count - 1
        head = lax.slice_in_dim(cells, 0, width, axis=dim)
        tail = lax.slice_in_dim(cells, cells.shape[dim] - width, cells.shape[dim], axis=dim)
        cells = jnp.concatenate(
            [
                lax.ppermute(tail, axis, [(i, (i + 1) % count) for i in range(ends)]),
                cells,
                lax.ppermute(head, axis, [((i + 1) % count, i) for i in range(ends)]),
            ],
            axis=dim,
        )
    return cells


def laplace_local(extended):
    padded = jnp.pad(extended, ((0, 0), (0, 0), (1, 1), (1, 1)))
    centre = padded[:, 1:-1, 1:-1, 1:-1]
    return (
        padded[:, 2:, 1:-1, 1:-1]
        + padded[:, :-2, 1:-1, 1:-1]
        + padded[:, 1:-1, 2:, 1:-1]
        + padded[:, 1:-1, :-2, 1:-1]
        + padded[:, 1:-1, 1:-1, 2:]
        + padded[:, 1:-1, 1:-1, :-2]
        - 6.0 * centre
    )


def advance_local(fields, pair_rates, member, active):
    squared = fields * fields
    partial_sums = jnp.einsum("pk,pxzy->kxzy", member, squared, precision=lax.Precision.HIGHEST)
    class_sums = lax.psum(partial_sums, "grp")
    summed = jnp.sum(class_sums, axis=0)
    inverse = 1.0 / (1.0 + summed)
    driving = jnp.einsum("pk,kxzy->pxzy", pair_rates, class_sums, precision=lax.Precision.HIGHEST)
    rates = driving * inverse[None]
    extended = extended_2(fields, (("slab", 1),), 1)
    potential = (
        -fields
        + fields * squared
        + 2.0 * coupling * fields * (summed[None] - squared)
        - stiffness * laplace_local(extended)
    )
    weighted = active[None] * rates
    numerator, raw_denominator = lax.psum(
        (jnp.sum(weighted * potential, axis=(1, 2, 3)), jnp.sum(weighted, axis=(1, 2, 3))), "slab"
    )
    lagrange = numerator / jnp.maximum(raw_denominator, 1.0)
    updated = fields - time_step * weighted * (potential - lagrange[:, None, None, None])
    return (updated, potential, class_sums, numerator, raw_denominator)


def retreat(
    state_adj_next,
    fields,
    potential,
    class_sums,
    numerator,
    raw_denominator,
    member,
    pair_rates,
    active,
):
    squared = fields * fields
    summed = jnp.sum(class_sums, axis=0)
    inverse = 1.0 / (1.0 + summed)
    driving = jnp.einsum("pk,kxzy->pxzy", pair_rates, class_sums, precision=lax.Precision.HIGHEST)
    rates = driving * inverse[None]
    weighted = active[None] * rates
    denominator = jnp.maximum(raw_denominator, 1.0)
    lagrange = numerator / denominator
    scaled = time_step * active[None] * state_adj_next
    first_part = scaled * rates
    lagrange_adj = lax.psum(jnp.sum(first_part, axis=(1, 2, 3)), "slab")
    numer_adj = lagrange_adj / denominator
    potential_adj = weighted * numer_adj[:, None, None, None] - first_part
    extended = extended_2(potential_adj, (("slab", 1),), 1)
    curvature = laplace_local(extended)
    denom_adj = jnp.where(
        raw_denominator > 1.0, -lagrange_adj * numerator / (denominator * denominator), 0.0
    )
    rate_adj = -scaled * (potential - lagrange[:, None, None, None]) + active[None] * (
        numer_adj[:, None, None, None] * potential + denom_adj[:, None, None, None]
    )
    drive_adj = rate_adj * inverse[None]
    state_adj = (
        state_adj_next
        + potential_adj
        * (
            -1.0
            + 3.0 * squared
            + 2.0 * coupling * (summed[None] - squared)
            - 4.0 * coupling * squared
        )
        - stiffness * curvature
    )
    weighted_sums = jnp.einsum(
        "pk,pxzy->kxzy", pair_rates, drive_adj, precision=lax.Precision.HIGHEST
    )
    shared_sum = jnp.sum(
        2.0 * coupling * potential_adj * fields - (inverse * inverse)[None] * rate_adj * driving,
        axis=0,
    )
    weighted_sums, shared_sum = lax.psum((weighted_sums, shared_sum), "grp")
    class_adj = weighted_sums + shared_sum[None]
    state_adj = state_adj + 2.0 * fields * jnp.einsum(
        "pk,kxzy->pxzy", member, class_adj, precision=lax.Precision.HIGHEST
    )
    products = jnp.einsum("pxzy,kxzy->pk", drive_adj, class_sums, precision=lax.Precision.HIGHEST)
    mobility_term = jnp.dot(member.T, products, precision=lax.Precision.HIGHEST)
    return (state_adj, mobility_term)


def on_device(initial, target, birth_step, classes, mobility):
    classes_count = mobility.shape[0]
    member = (classes[:, None] == jnp.arange(classes_count, dtype=jnp.int32)[None, :]).astype(
        jnp.float32
    )
    pair_rates = jnp.dot(member, mobility, precision=lax.Precision.HIGHEST)
    fields = initial
    stored = []
    for step_index in range(STEPS):
        active = (birth_step <= step_index).astype(jnp.float32)
        updated, potential, class_sums, numerator, raw_denominator = advance_local(
            fields, pair_rates, member, active
        )
        stored.append((fields, potential, class_sums, numerator, raw_denominator, active))
        fields = updated
    state_adj = fields - target
    mobility_acc = jnp.zeros((classes_count, classes_count), jnp.float32)
    for step_index in range(STEPS - 1, -1, -1):
        saved_fields, potential, class_sums, numerator, raw_denominator, active = stored[step_index]
        state_adj, mobility_term = retreat(
            state_adj,
            saved_fields,
            potential,
            class_sums,
            numerator,
            raw_denominator,
            member,
            pair_rates,
            active,
        )
        mobility_acc = mobility_acc + mobility_term
    mobility_total = lax.psum(mobility_acc, ("slab", "grp"))
    scale = time_step * (initial.shape[1] * lax.axis_size("slab")) * initial.shape[2]
    return (fields, state_adj, mobility_total / scale)


def solution(mesh):
    return jax.shard_map(
        on_device,
        mesh=mesh,
        in_specs=(
            P("grp", "slab", None, None),
            P("grp", "slab", None, None),
            P("slab", None, None),
            P("grp"),
            P(),
        ),
        out_specs=(P("grp", "slab", None, None), P("grp", "slab", None, None), P()),
        check_vma=False,
    )
```

profile of v0, /device:TPU:0, one launch (start us, length us, event | category | flops | bytes accessed | tf_op | source)
XLA Modules:
  0.0 990.1 jit_solution(4415834130746513272)
XLA Ops:
  7.2 1.4 copy.20
  8.7 3.6 collective-permute-start.1
  13.7 1.8 fusion.9
  20.0 60.5 %all-reduce.25.cloned.1.call-done = f32[4,4,32,256]{3,0,2,1:T(4,128)} async-done(((f32[4,4,32,256]{3,0,2,1:T(4,128)}), f32[4,4,32,256]{3,0,2,1:T(4,128)}) %all-reduce.25.cloned.1.call-update) | async-done | bytes 524304 | tf_op jit(solution)/shard_map/psum | solution.py:46
  80.5 1.4 reduce_sum.196
  82.6 3.1 fusion.134
  85.7 40.3 %all-reduce.11 = (f32[4]{0:T(128)S(1)}, f32[4]{0:T(128)S(1)}) all-reduce(f32[4]{0:T(128)S(1)} %get-tuple-element.13, f32[4]{0:T(128)S(1)} %get-tuple-element.12), channel_id=1, replica_groups=mesh['slab'=16,'grp'=8] {'slab'}, use_global_device_ids=true, to_apply=%region_3.4 | all-reduce | flops 8 | bytes 64 | tf_op jit(solution)/shard_map/psum | solution.py:59
  126.6 1.7 multiply_subtract_fusion.11
  130.9 1.6 fusion.7
  132.6 3.9 collective-permute-done.2
  136.5 1.8 select_maximum_fusion.12
  138.2 52.1 %all-reduce.27.cloned.1.call-done = f32[4,4,32,256]{3,0,2,1:T(4,128)} async-done(((f32[4,4,32,256]{3,0,2,1:T(4,128)}), f32[4,4,32,256]{3,0,2,1:T(4,128)}) %all-reduce.27.cloned.1.call-update) | async-done | bytes 524304 | tf_op jit(solution)/shard_map/psum | solution.py:46
  190.3 1.4 reduce_sum.199
  192.4 4.1 fusion.135
  196.5 40.3 %all-reduce.10 = (f32[4]{0:T(128)S(1)}, f32[4]{0:T(128)S(1)}) all-reduce(f32[4]{0:T(128)S(1)} %get-tuple-element.11, f32[4]{0:T(128)S(1)} %get-tuple-element.10), channel_id=1, replica_groups=mesh['slab'=16,'grp'=8] {'slab'}, use_global_device_ids=true, to_apply=%region_9.10 | all-reduce | flops 8 | bytes 64 | tf_op jit(solution)/shard_map/psum | solution.py:59
  240.4 1.6 fusion.5
  242.2 3.7 collective-permute-done.4
  245.9 1.8 select_maximum_fusion.10
  247.7 52.0 %all-reduce.29.cloned.1.call-done = f32[4,4,32,256]{3,0,2,1:T(4,128)} async-done(((f32[4,4,32,256]{3,0,2,1:T(4,128)}), f32[4,4,32,256]{3,0,2,1:T(4,128)}) %all-reduce.29.cloned.1.call-update) | async-done | bytes 524304 | tf_op jit(solution)/shard_map/psum | solution.py:46
  299.7 1.4 reduce_sum.202
  301.8 4.6 fusion.136
  306.4 40.4 %all-reduce.9 = (f32[4]{0:T(128)S(1)}, f32[4]{0:T(128)S(1)}) all-reduce(f32[4]{0:T(128)} %get-tuple-element.9, f32[4]{0:T(128)} %get-tuple-element.8), channel_id=1, replica_groups=mesh['slab'=16,'grp'=8] {'slab'}, use_global_device_ids=true, to_apply=%region_15.16 | all-reduce | flops 8 | bytes 64 | tf_op jit(solution)/shard_map/psum | solution.py:59
  352.0 1.6 fusion.3
  353.7 4.0 collective-permute-done.6
  357.7 1.8 select_maximum_fusion.8
  359.5 51.8 %all-reduce.31.cloned.1.call-done = f32[4,4,32,256]{3,0,2,1:T(4,128)} async-done(((f32[4,4,32,256]{3,0,2,1:T(4,128)}), f32[4,4,32,256]{3,0,2,1:T(4,128)}) %all-reduce.31.cloned.1.call-update) | async-done | bytes 524304 | tf_op jit(solution)/shard_map/psum | solution.py:46
  411.3 1.4 reduce_sum.205
  413.4 5.4 fusion.137
  418.8 40.4 %all-reduce.8 = (f32[4]{0:T(128)S(1)}, f32[4]{0:T(128)S(1)}) all-reduce(f32[4]{0:T(128)} %get-tuple-element.7, f32[4]{0:T(128)} %get-tuple-element.6), channel_id=1, replica_groups=mesh['slab'=16,'grp'=8] {'slab'}, use_global_device_ids=true, to_apply=%region_21.22 | all-reduce | flops 8 | bytes 64 | tf_op jit(solution)/shard_map/psum | solution.py:59
  459.3 3.1 fusion.126
  462.4 35.5 %psum.187 = f32[4]{0:T(128)S(1)} all-reduce(f32[4]{0:T(128)S(1)} %get-tuple-element.48), channel_id=1, replica_groups=mesh['slab'=16,'grp'=8] {'slab'}, use_global_device_ids=true, to_apply=%region_25.26 | all-reduce | flops 4 | bytes 32 | tf_op jit(solution)/shard_map/psum | solution.py:88
  497.9 3.3 subtract_reduce_fusion.3
  501.9 4.5 collective-permute-start.9
  507.7 2.0 fusion.87
  511.0 3.6 convolution_bitcast_fusion.3
  515.5 2.7 select_maximum_fusion.6
  518.2 50.4 %all-reduce.39.cloned.1.call-done = (f32[4,4,32,256]{3,0,2,1:T(4,128)}, f32[4,32,256]{2,1,0:T(8,128)}) async-done(((f32[4,4,32,256]{3,0,2,1:T(4,128)}, f32[4,32,256]{2,1,0:T(8,128)}), (f32[4,4,32,256]{3,0,2,1:T(4,128)}, f32[4,32,256]{2,1,0:T(8,128)})) %all-reduce.39.cloned.1.call-update) | async-done | bytes 655376 | tf_op jit(solution)/shard_map/psum | solution.py:118
  568.6 6.0 fusion.127
  574.6 40.4 %psum.190 = f32[4]{0:T(128)S(1)} all-reduce(f32[4]{0:T(128)} %get-tuple-element.99), channel_id=1, replica_groups=mesh['slab'=16,'grp'=8] {'slab'}, use_global_device_ids=true, to_apply=%region_30.31 | all-reduce | flops 4 | bytes 32 | tf_op jit(solution)/shard_map/psum | solution.py:88
  615.7 3.0 subtract_reduce_fusion.2
  619.5 1.9 collective-permute-start.11
  622.7 2.0 fusion.84
  624.8 2.5 convolution_bitcast_fusion.2
  627.3 1.6 convolution_add_fusion.2
  628.9 2.7 select_maximum_fusion.4
  631.7 51.4 %all-reduce.37.cloned.1.call-done = (f32[4,4,32,256]{3,0,2,1:T(4,128)}, f32[4,32,256]{2,1,0:T(8,128)}) async-done(((f32[4,4,32,256]{3,0,2,1:T(4,128)}, f32[4,32,256]{2,1,0:T(8,128)}), (f32[4,4,32,256]{3,0,2,1:T(4,128)}, f32[4,32,256]{2,1,0:T(8,128)})) %all-reduce.37.cloned.1.call-update) | async-done | bytes 655376 | tf_op jit(solution)/shard_map/psum | solution.py:118
  683.1 5.8 fusion.128
  688.9 40.8 %psum.193 = f32[4]{0:T(128)S(1)} all-reduce(f32[4]{0:T(128)} %get-tuple-element.101), channel_id=1, replica_groups=mesh['slab'=16,'grp'=8] {'slab'}, use_global_device_ids=true, to_apply=%region_35.36 | all-reduce | flops 4 | bytes 32 | tf_op jit(solution)/shard_map/psum | solution.py:88
  730.3 2.9 subtract_reduce_fusion.1
  733.2 1.4 collective-permute-start.13
  736.0 2.0 fusion.81
  738.1 2.5 convolution_bitcast_fusion.1
  740.6 1.6 convolution_add_fusion.1
  742.2 1.8 select_maximum_fusion.2
  744.0 52.3 %all-reduce.35.cloned.1.call-done = (f32[4,4,32,256]{3,0,2,1:T(4,128)}, f32[4,32,256]{2,1,0:T(8,128)}) async-done(((f32[4,4,32,256]{3,0,2,1:T(4,128)}, f32[4,32,256]{2,1,0:T(8,128)}), (f32[4,4,32,256]{3,0,2,1:T(4,128)}, f32[4,32,256]{2,1,0:T(8,128)})) %all-reduce.35.cloned.1.call-update) | async-done | bytes 655376 | tf_op jit(solution)/shard_map/psum | solution.py:118
  796.3 5.8 fusion.129
  802.1 40.4 %psum.196 = f32[4]{0:T(128)S(1)} all-reduce(f32[4]{0:T(128)} %get-tuple-element.103), channel_id=1, replica_groups=mesh['slab'=16,'grp'=8] {'slab'}, use_global_device_ids=true, to_apply=%region_40.41 | all-reduce | flops 4 | bytes 32 | tf_op jit(solution)/shard_map/psum | solution.py:88
  843.3 3.0 subtract_reduce_fusion
  846.3 2.5 convolution_bitcast_fusion
  849.1 2.0 fusion.78
  851.1 62.5 %psum.199 = f32[4,4]{1,0:T(4,128)S(1)} all-reduce(f32[4,4]{1,0:T(4,128)S(1)} %convolution_add_fusion), channel_id=1, replica_groups=mesh['slab'=16,'grp'=8] {'slab','grp'}, use_global_device_ids=true, to_apply=%region_44.45 | all-reduce | flops 16 | bytes 128 | tf_op jit(solution)/shard_map/psum | solution.py:159
  917.6 4.4 collective-permute-done.14
  922.6 56.6 %all-reduce.33.cloned.1.call-done = (f32[4,4,32,256]{3,0,2,1:T(4,128)}, f32[4,32,256]{2,1,0:T(8,128)}) async-done(((f32[4,4,32,256]{3,0,2,1:T(4,128)}, f32[4,32,256]{2,1,0:T(8,128)}), (f32[4,4,32,256]{3,0,2,1:T(4,128)}, f32[4,32,256]{2,1,0:T(8,128)})) %all-reduce.33.cloned.1.call-update) | async-done | bytes 655376 | tf_op jit(solution)/shard_map/psum | solution.py:118
  979.2 3.0 fusion.20
  (177 shorter events, 36.1 us)
Async XLA Ops:
  7.2 12.0 %copy-start = (f32[4,4]{1,0:T(4,128)S(1)}, f32[4,4]{1,0:T(4,128)}, u32[]{:S(2)}) copy-start(f32[4,4]{1,0:T(4,128)} %param.9) | copy-start | bytes 196
  7.2 6.5 copy-start.1
  7.2 6.5 copy-start.40
  7.2 73.3 %all-reduce.25.cloned.1.call-start = ((), (), s32[]{:S(2)}) async-start(), calls=%async_computation | async-start | bytes 1048576 | tf_op jit(solution)/shard_map/psum | solution.py:46
  8.7 6.9 copy-start.39
  8.7 10.6 %collective-permute-start.1 = (f32[4,1,32,256]{3,0,2,1:T(4,128)S(1)}, f32[4,1,32,256]{3,0,2,1:T(4,128)S(1)}, u32[]{:S(2)}, u32[]{:S(2)}) collective-permute-start(f32[4,1,32,256]{3,0,2,1:T(4,128)S(1)} %get-tuple-element.71), channel_id=1, source_target_pairs={{0,8},{8,16},{16,24},{24,32},{32,40},{40,48},{48,56},{56,64},{64,7... | collective-permute-start | bytes 393224 | tf_op jit(solution)/shard_map/ppermute | solution.py:20
  12.4 7.0 collective-permute-start
  15.5 174.8 %all-reduce.27.cloned.1.call-start = ((), (), s32[]{:S(2)}) async-start(), calls=%async_computation.1 | async-start | bytes 1048576 | tf_op jit(solution)/shard_map/psum | solution.py:46
  19.3 61.2 %copy-start.35 = (f32[4,1,32,256]{3,0,2,1:T(4,128)}, f32[4,1,32,256]{3,0,2,1:T(4,128)S(1)}, u32[]{:S(2)}) copy-start(f32[4,1,32,256]{3,0,2,1:T(4,128)S(1)} %collective-permute-done.1) | copy-start | bytes 393220
  85.7 42.6 %copy-start.5 = (f32[4,4,32,256]{3,0,2,1:T(4,128)}, f32[4,4,32,256]{3,0,2,1:T(4,128)S(1)}, u32[]{:S(2)}) copy-start(f32[4,4,32,256]{3,0,2,1:T(4,128)S(1)} %get-tuple-element.56) | copy-start | bytes 1572868
  85.7 42.6 %copy-start.7 = (f32[4,4,32,256]{3,0,2,1:T(4,128)}, f32[4,4,32,256]{3,0,2,1:T(4,128)S(1)}, u32[]{:S(2)}) copy-start(f32[4,4,32,256]{3,0,2,1:T(4,128)S(1)} %get-tuple-element.95) | copy-start | bytes 1572868
  128.3 4.3 collective-permute-start.3
  129.6 6.9 collective-permute-start.2
  132.5 59.8 %copy-start.21 = (f32[4,32,256]{2,1,0:T(8,128)S(1)}, f32[4,32,256]{2,1,0:T(8,128)}, u32[]{:S(2)}) copy-start(f32[4,32,256]{2,1,0:T(8,128)} %convert_element_type.23) | copy-start | bytes 393220
  132.6 167.1 %all-reduce.29.cloned.1.call-start = ((), (), s32[]{:S(2)}) async-start(), calls=%async_computation.2 | async-start | bytes 1048576 | tf_op jit(solution)/shard_map/psum | solution.py:46
  191.7 4.8 copy-start.30
  196.5 41.3 %copy-start.10 = (f32[4,4,32,256]{3,0,2,1:T(4,128)}, f32[4,4,32,256]{3,0,2,1:T(4,128)S(1)}, u32[]{:S(2)}) copy-start(f32[4,4,32,256]{3,0,2,1:T(4,128)S(1)} %get-tuple-element.55) | copy-start | bytes 1572868
  196.5 41.3 %copy-start.12 = (f32[4,4,32,256]{3,0,2,1:T(4,128)}, f32[4,4,32,256]{3,0,2,1:T(4,128)S(1)}, u32[]{:S(2)}) copy-start(f32[4,4,32,256]{3,0,2,1:T(4,128)S(1)} %get-tuple-element.96) | copy-start | bytes 1572868
  237.8 4.5 collective-permute-start.5
  239.1 6.9 collective-permute-start.4
  242.0 59.8 %copy-start.22 = (f32[4,32,256]{2,1,0:T(8,128)S(1)}, f32[4,32,256]{2,1,0:T(8,128)}, u32[]{:S(2)}) copy-start(f32[4,32,256]{2,1,0:T(8,128)} %convert_element_type.24) | copy-start | bytes 393220
  242.0 169.3 %all-reduce.31.cloned.1.call-start = ((), (), s32[]{:S(2)}) async-start(), calls=%async_computation.3 | async-start | bytes 1048576 | tf_op jit(solution)/shard_map/psum | solution.py:46
  301.0 5.3 copy-start.32
  306.4 43.0 %copy-start.15 = (f32[4,4,32,256]{3,0,2,1:T(4,128)}, f32[4,4,32,256]{3,0,2,1:T(4,128)S(1)}, u32[]{:S(2)}) copy-start(f32[4,4,32,256]{3,0,2,1:T(4,128)S(1)} %get-tuple-element.54) | copy-start | bytes 1572868
  306.4 43.0 %copy-start.17 = (f32[4,4,32,256]{3,0,2,1:T(4,128)}, f32[4,4,32,256]{3,0,2,1:T(4,128)S(1)}, u32[]{:S(2)}) copy-start(f32[4,4,32,256]{3,0,2,1:T(4,128)S(1)} %get-tuple-element.97) | copy-start | bytes 1572868
  349.4 4.3 collective-permute-start.7
  350.7 7.1 collective-permute-start.6
  353.6 59.7 %copy-start.23 = (f32[4,32,256]{2,1,0:T(8,128)S(1)}, f32[4,32,256]{2,1,0:T(8,128)}, u32[]{:S(2)}) copy-start(f32[4,32,256]{2,1,0:T(8,128)} %convert_element_type.25) | copy-start | bytes 393220
  353.6 215.0 %all-reduce.39.cloned.1.call-start = ((), (), s32[]{:S(2)}) async-start(), calls=%async_computation.7 | async-start | bytes 1310720 | tf_op jit(solution)/shard_map/psum | solution.py:118
  353.7 57.6 %copy-start.37 = (f32[4,1,32,256]{3,0,2,1:T(4,128)}, f32[4,1,32,256]{3,0,2,1:T(4,128)S(1)}, u32[]{:S(2)}) copy-start(f32[4,1,32,256]{3,0,2,1:T(4,128)S(1)} %collective-permute-done.7) | copy-start | bytes 393220
  357.7 54.9 %copy-start.38 = (f32[4,1,32,256]{3,0,2,1:T(4,128)}, f32[4,1,32,256]{3,0,2,1:T(4,128)S(1)}, u32[]{:S(2)}) copy-start(f32[4,1,32,256]{3,0,2,1:T(4,128)S(1)} %collective-permute-done.6) | copy-start | bytes 393220
  412.7 6.1 copy-start.33
  413.4 45.9 %copy-start.2 = (f32[4,32,256]{2,1,0:T(8,128)}, f32[4,32,256]{2,1,0:T(8,128)S(1)}, u32[]{:S(2)}) copy-start(f32[4,32,256]{2,1,0:T(8,128)S(1)} %get-tuple-element.80) | copy-start | bytes 393220
  413.4 45.9 %copy-start.24 = (f32[4,32,256]{2,1,0:T(8,128)S(1)}, f32[4,32,256]{2,1,0:T(8,128)}, u32[]{:S(2)}) copy-start(f32[4,32,256]{2,1,0:T(8,128)} %get-tuple-element.51) | copy-start | bytes 393220
  418.8 43.6 %copy-start.19 = (f32[4,4,32,256]{3,0,2,1:T(4,128)}, f32[4,4,32,256]{3,0,2,1:T(4,128)S(1)}, u32[]{:S(2)}) copy-start(f32[4,4,32,256]{3,0,2,1:T(4,128)S(1)} %get-tuple-element.53) | copy-start | bytes 1572868
  459.2 3.1 copy-start.43
  497.9 9.8 copy-start.3
  501.2 8.6 copy-start.18
  501.9 13.6 %collective-permute-start.9 = (f32[4,1,32,256]{3,0,2,1:T(4,128)}, f32[4,1,32,256]{3,0,2,1:T(4,128)}, u32[]{:S(2)}, u32[]{:S(2)}) collective-permute-start(f32[4,1,32,256]{3,0,2,1:T(4,128)} %get-tuple-element.63), channel_id=1, source_target_pairs={{0,8},{8,16},{16,24},{24,32},{32,40},{40,48},{48,56},{56,64},{64,7... | collective-permute-start | bytes 393224 | tf_op jit(solution)/shard_map/ppermute | solution.py:20
  506.4 9.0 collective-permute-start.8
  510.7 172.4 %all-reduce.37.cloned.1.call-start = ((), (), s32[]{:S(2)}) async-start(), calls=%async_computation.6 | async-start | bytes 1310720 | tf_op jit(solution)/shard_map/psum | solution.py:118
  568.6 47.1 %copy-start.16 = (f32[4,4,32,256]{3,0,2,1:T(4,128)S(1)}, f32[4,4,32,256]{3,0,2,1:T(4,128)}, u32[]{:S(2)}) copy-start(f32[4,4,32,256]{3,0,2,1:T(4,128)} %copy-done.15) | copy-start | bytes 1572868
  618.7 6.1 copy-start.14
  619.5 9.5 collective-permute-start.11
  621.4 7.5 collective-permute-start.10
  624.8 171.5 %all-reduce.35.cloned.1.call-start = ((), (), s32[]{:S(2)}) async-start(), calls=%async_computation.5 | async-start | bytes 1310720 | tf_op jit(solution)/shard_map/psum | solution.py:118
  627.3 55.8 %copy-start.13 = (f32[4,4,32,256]{3,0,2,1:T(4,128)S(1)}, f32[4,4,32,256]{3,0,2,1:T(4,128)}, u32[]{:S(2)}) copy-start(f32[4,4,32,256]{3,0,2,1:T(4,128)} %copy-done.12) | copy-start | bytes 1572868
  627.3 55.8 %copy-start.29 = (f32[4,32,256]{2,1,0:T(8,128)S(1)}, f32[4,32,256]{2,1,0:T(8,128)}, u32[]{:S(2)}) copy-start(f32[4,32,256]{2,1,0:T(8,128)} %get-tuple-element.81) | copy-start | bytes 393220
  683.1 47.2 %copy-start.11 = (f32[4,4,32,256]{3,0,2,1:T(4,128)S(1)}, f32[4,4,32,256]{3,0,2,1:T(4,128)}, u32[]{:S(2)}) copy-start(f32[4,4,32,256]{3,0,2,1:T(4,128)} %copy-done.10) | copy-start | bytes 1572868
  733.2 4.9 copy-start.9
  733.2 9.0 collective-permute-start.13
  734.7 7.6 collective-permute-start.12
  738.0 241.2 %all-reduce.33.cloned.1.call-start = ((), (), s32[]{:S(2)}) async-start(), calls=%async_computation.4 | async-start | bytes 1310720 | tf_op jit(solution)/shard_map/psum | solution.py:118
  740.6 55.7 %copy-start.8 = (f32[4,4,32,256]{3,0,2,1:T(4,128)S(1)}, f32[4,4,32,256]{3,0,2,1:T(4,128)}, u32[]{:S(2)}) copy-start(f32[4,4,32,256]{3,0,2,1:T(4,128)} %copy-done.7) | copy-start | bytes 1572868
  740.6 55.7 %copy-start.28 = (f32[4,32,256]{2,1,0:T(8,128)S(1)}, f32[4,32,256]{2,1,0:T(8,128)}, u32[]{:S(2)}) copy-start(f32[4,32,256]{2,1,0:T(8,128)} %get-tuple-element.83) | copy-start | bytes 393220
  740.6 55.7 %copy-start.31 = (f32[4,32,256]{2,1,0:T(8,128)S(1)}, f32[4,32,256]{2,1,0:T(8,128)}, u32[]{:S(2)}) copy-start(f32[4,32,256]{2,1,0:T(8,128)} %copy-done.30) | copy-start | bytes 393220
  796.3 46.9 %copy-start.6 = (f32[4,4,32,256]{3,0,2,1:T(4,128)S(1)}, f32[4,4,32,256]{3,0,2,1:T(4,128)}, u32[]{:S(2)}) copy-start(f32[4,4,32,256]{3,0,2,1:T(4,128)} %copy-done.5) | copy-start | bytes 1572868
  796.3 46.9 %copy-start.20 = (f32[4,32,256]{2,1,0:T(8,128)S(1)}, f32[4,32,256]{2,1,0:T(8,128)}, u32[]{:S(2)}) copy-start(f32[4,32,256]{2,1,0:T(8,128)} %convert_element_type.22) | copy-start | bytes 393220
  796.3 46.9 %copy-start.25 = (f32[4,32,256]{2,1,0:T(8,128)S(1)}, f32[4,32,256]{2,1,0:T(8,128)}, u32[]{:S(2)}) copy-start(f32[4,32,256]{2,1,0:T(8,128)} %get-tuple-element.73) | copy-start | bytes 393220
  843.3 5.6 copy-start.50
  913.7 3.9 collective-permute-start.15
  915.0 7.0 collective-permute-start.14
  916.3 62.9 %copy-start.27 = (f32[4,32,256]{2,1,0:T(8,128)S(1)}, f32[4,32,256]{2,1,0:T(8,128)}, u32[]{:S(2)}) copy-start(f32[4,32,256]{2,1,0:T(8,128)} %copy-done.26) | copy-start | bytes 393220
  916.3 62.9 %copy-start.34 = (f32[4,4,32,256]{3,0,2,1:T(4,128)S(1)}, f32[4,4,32,256]{3,0,2,1:T(4,128)}, u32[]{:S(2)}) copy-start(f32[4,4,32,256]{3,0,2,1:T(4,128)} %get-tuple-element.104) | copy-start | bytes 1572868
  (11 other events, 10.8 us)
Sparse Core Ops, SparseCore 0:
  15.7 64.7 all-reduce.24
  132.7 57.5 all-reduce.26
  242.1 57.5 all-reduce.28
  353.7 57.5 all-reduce.30
  510.8 57.7 all-reduce.38
  624.9 58.1 all-reduce.36
  738.1 58.1 all-reduce.34
  916.5 62.6 all-reduce.32
where the time goes:
time: 999 us; the launch traced here: 990 us
  waiting for transfers between devices  444 us (44%)
  blocking collectives  381 us (38%)
  matrix products  68.3 us (7%)
  other arithmetic  46.8 us (5%)
  starting transfers between devices  27.8 us (3%)
  between operations  15 us (2%)
    psum x4, waiting for transfers between devices, advance_local(): class_sums = lax.psum(partial_sums, 'grp')  216 us
    psum x4, waiting for transfers between devices, retreat(): weighted_sums, shared_sum = lax.psum((weighted_sums, shared_sum), 'grp')  211 us
    psum x4, blocking collectives, advance_local(): lax.psum((jnp.sum(weighted * potential, axis=(1, 2, 3)), jnp.sum(weighted...  162 us
    psum x4, blocking collectives, retreat(): lagrange_adj = lax.psum(jnp.sum(first_part, axis=(1, 2, 3)), 'slab')  157 us
    psum x1, blocking collectives, on_device(): mobility_total = lax.psum(mobility_acc, ('slab', 'grp'))  62.5 us
    dot_general x4, matrix products, retreat(): jnp.einsum('pk,kxzy->pxzy', member, class_adj, precision=lax.Precision.HI...  20.6 us
  transfers between devices with their start and end apart: 24, of which 13 were waited for; matrix products, arithmetic and copies ran while one was open for 4% of the time, Pallas kernels for 0%

commit v1 on v0

--- a/solution.py
+++ b/solution.py
@@ -43,7 +43,11 @@
 def advance_local(fields, pair_rates, member, active):
     squared = fields * fields
     partial_sums = jnp.einsum("pk,pxzy->kxzy", member, squared, precision=lax.Precision.HIGHEST)
-    class_sums = lax.psum(partial_sums, "grp")
+    class_sums = partial_sums
+    for hop in (1, 2, 4):
+        class_sums = class_sums + lax.ppermute(
+            class_sums, "grp", [(dev, dev ^ hop) for dev in range(8)]
+        )
     summed = jnp.sum(class_sums, axis=0)
     inverse = 1.0 / (1.0 + summed)
     driving = jnp.einsum("pk,kxzy->pxzy", pair_rates, class_sums, precision=lax.Precision.HIGHEST)

time: 999 us -> 850 us (0.85)
  waiting for transfers between devices: 444 us -> 313 us
  starting transfers between devices: 27.8 us -> 47.8 us
  other arithmetic: 46.8 us -> 34.9 us
  matrix products: 68.3 us -> 56.5 us
  blocking collectives: 381 us -> 371 us
    psum x4 -> x0, waiting for transfers between devices: 216 us -> none  [advance_local(): class_sums = lax.psum(partial_sums, 'grp')]
    ppermute x0 -> x12, waiting for transfers between devices: none -> 66.6 us  [advance_local(): lax.ppermute(class_sums, 'grp', [(dev, dev ^ hop) for dev in range(8)])]
    ppermute x0 -> x12, starting transfers between devices: none -> 20.3 us  [advance_local(): lax.ppermute(class_sums, 'grp', [(dev, dev ^ hop) for dev in range(8)])]
    ppermute x8, waiting for transfers between devices: 15.9 us -> 29.1 us  [extended_2(): lax.ppermute(head, axis, [((i + 1) % count, i) for i in range(ends)])]
    psum x4, blocking collectives: 162 us -> 149 us  [advance_local(): lax.psum((jnp.sum(weighted * potential, axis=(1, 2, 3)), jnp.sum(weighted...]
  transfers between devices with their start and end apart: 24 -> 32, of which waited for: 13 -> 27; matrix products, arithmetic and copies ran while one was open for 4% -> 2% of each run, Pallas kernels for 0% -> 0%
where the time goes in v1:
time: 850 us; the launch traced here: 841 us
  blocking collectives  371 us (44%)
  waiting for transfers between devices  313 us (37%)
  matrix products  56.5 us (7%)
  starting transfers between devices  47.8 us (6%)
  other arithmetic  34.9 us (4%)
  between operations  14.9 us (2%)
    psum x4, waiting for transfers between devices, retreat(): weighted_sums, shared_sum = lax.psum((weighted_sums, shared_sum), 'grp')  213 us
    psum x4, blocking collectives, retreat(): lagrange_adj = lax.psum(jnp.sum(first_part, axis=(1, 2, 3)), 'slab')  159 us
    psum x4, blocking collectives, advance_local(): lax.psum((jnp.sum(weighted * potential, axis=(1, 2, 3)), jnp.sum(weighted...  149 us
    ppermute x12, waiting for transfers between devices, advance_local(): lax.ppermute(class_sums, 'grp', [(dev, dev ^ hop) for dev in range(8)])  66.6 us
    psum x1, blocking collectives, on_device(): mobility_total = lax.psum(mobility_acc, ('slab', 'grp'))  62.4 us
    ppermute x8, waiting for transfers between devices, extended_2(): lax.ppermute(head, axis, [((i + 1) % count, i) for i in range(ends)])  29.1 us
    dot_general x4, matrix products, retreat(): jnp.einsum('pk,kxzy->pxzy', member, class_adj, precision=lax.Precision.HI...  20.5 us
    ppermute x12, starting transfers between devices, advance_local(): lax.ppermute(class_sums, 'grp', [(dev, dev ^ hop) for dev in range(8)])  20.3 us
  transfers between devices with their start and end apart: 32, of which 27 were waited for; matrix products, arithmetic and copies ran while one was open for 2% of the time, Pallas kernels for 0%

profile of v1, /device:TPU:0, one launch (start us, length us, event | category | flops | bytes accessed | tf_op | source)
XLA Modules:
  0.0 841.1 jit_solution(1333441476727551224)
XLA Ops:
  7.2 2.1 fusion.9
  9.5 1.9 collective-permute-done
  11.5 2.1 collective-permute-start.1
  14.0 3.5 collective-permute-start.4
  18.9 7.0 collective-permute-done.1
  26.0 3.8 collective-permute-start.2
  31.5 9.6 %collective-permute-done.2 = f32[4,4,32,256]{3,0,2,1:T(4,128)S(1)} collective-permute-done((f32[4,4,32,256]{3,0,2,1:T(4,128)S(1)}, f32[4,4,32,256]{3,0,2,1:T(4,128)S(1)}, u32[]{:S(2)}, u32[]{:S(2)}) %collective-permute-start.2) | collective-permute-done | bytes 524320 | tf_op jit(solution)/shard_map/ppermute | solution.py:48
  42.3 1.9 fusion.134
  44.2 40.7 %all-reduce.11 = (f32[4]{0:T(128)S(1)}, f32[4]{0:T(128)S(1)}) all-reduce(f32[4]{0:T(128)S(1)} %get-tuple-element.13, f32[4]{0:T(128)S(1)} %get-tuple-element.12), channel_id=1, replica_groups=mesh['slab'=16,'grp'=8] {'slab'}, use_global_device_ids=true, to_apply=%region_2.3 | all-reduce | flops 8 | bytes 64 | tf_op jit(solution)/shard_map/psum | solution.py:63
  86.5 1.9 collective-permute-done.5
  90.0 12.7 %collective-permute-done.6 = f32[4,4,32,256]{3,0,2,1:T(4,128)S(1)} collective-permute-done((f32[4,4,32,256]{3,0,2,1:T(4,128)S(1)}, f32[4,4,32,256]{3,0,2,1:T(4,128)S(1)}, u32[]{:S(2)}, u32[]{:S(2)}) %collective-permute-start.6) | collective-permute-done | bytes 524320 | tf_op jit(solution)/shard_map/ppermute | solution.py:48
  102.8 3.3 collective-permute-start.7
  109.9 4.4 collective-permute-done.8
  115.0 2.5 collective-permute-done.7
  118.7 1.9 fusion.135
  120.6 35.7 %all-reduce.10 = (f32[4]{0:T(128)S(1)}, f32[4]{0:T(128)S(1)}) all-reduce(f32[4]{0:T(128)S(1)} %get-tuple-element.11, f32[4]{0:T(128)S(1)} %get-tuple-element.10), channel_id=1, replica_groups=mesh['slab'=16,'grp'=8] {'slab'}, use_global_device_ids=true, to_apply=%region_7.8 | all-reduce | flops 8 | bytes 64 | tf_op jit(solution)/shard_map/psum | solution.py:63
  157.6 1.9 collective-permute-done.10
  161.0 12.7 %collective-permute-done.11 = f32[4,4,32,256]{3,0,2,1:T(4,128)S(1)} collective-permute-done((f32[4,4,32,256]{3,0,2,1:T(4,128)S(1)}, f32[4,4,32,256]{3,0,2,1:T(4,128)S(1)}, u32[]{:S(2)}, u32[]{:S(2)}) %collective-permute-start.11) | collective-permute-done | bytes 524320 | tf_op jit(solution)/shard_map/ppermute | solution.py:48
  173.8 3.3 collective-permute-start.12
  177.2 3.9 collective-permute-start.14
  183.6 4.4 collective-permute-done.13
  189.8 2.4 fusion.136
  192.2 37.5 %all-reduce.9 = (f32[4]{0:T(128)S(1)}, f32[4]{0:T(128)S(1)}) all-reduce(f32[4]{0:T(128)} %get-tuple-element.9, f32[4]{0:T(128)S(1)} %get-tuple-element.8), channel_id=1, replica_groups=mesh['slab'=16,'grp'=8] {'slab'}, use_global_device_ids=true, to_apply=%region_12.13 | all-reduce | flops 8 | bytes 64 | tf_op jit(solution)/shard_map/psum | solution.py:63
  232.5 1.9 collective-permute-done.15
  235.9 12.7 %collective-permute-done.16 = f32[4,4,32,256]{3,0,2,1:T(4,128)S(1)} collective-permute-done((f32[4,4,32,256]{3,0,2,1:T(4,128)S(1)}, f32[4,4,32,256]{3,0,2,1:T(4,128)S(1)}, u32[]{:S(2)}, u32[]{:S(2)}) %collective-permute-start.16) | collective-permute-done | bytes 524320 | tf_op jit(solution)/shard_map/ppermute | solution.py:48
  248.7 3.4 collective-permute-start.17
  252.1 1.9 collective-permute-start.19
  256.5 4.4 collective-permute-done.18
  261.5 1.9 collective-permute-done.17
  263.9 3.3 fusion.137
  267.3 35.7 %all-reduce.8 = (f32[4]{0:T(128)S(1)}, f32[4]{0:T(128)S(1)}) all-reduce(f32[4]{0:T(128)} %get-tuple-element.7, f32[4]{0:T(128)S(1)} %get-tuple-element.6), channel_id=1, replica_groups=mesh['slab'=16,'grp'=8] {'slab'}, use_global_device_ids=true, to_apply=%region_17.18 | all-reduce | flops 8 | bytes 64 | tf_op jit(solution)/shard_map/psum | solution.py:63
  303.0 3.3 fusion.126
  306.3 37.6 %psum.155 = f32[4]{0:T(128)S(1)} all-reduce(f32[4]{0:T(128)S(1)} %get-tuple-element.48), channel_id=1, replica_groups=mesh['slab'=16,'grp'=8] {'slab'}, use_global_device_ids=true, to_apply=%region_21.22 | all-reduce | flops 4 | bytes 32 | tf_op jit(solution)/shard_map/psum | solution.py:92
  343.9 3.2 subtract_reduce_fusion.3
  347.0 2.5 convolution_bitcast_fusion.3
  349.5 2.0 fusion.87
  351.6 2.0 collective-permute-start.21
  356.8 3.7 collective-permute-done.20
  362.2 54.3 %all-reduce.27.cloned.1.call-done = (f32[4,4,32,256]{3,0,2,1:T(4,128)}, f32[4,32,256]{2,1,0:T(8,128)}) async-done(((f32[4,4,32,256]{3,0,2,1:T(4,128)}, f32[4,32,256]{2,1,0:T(8,128)}), (f32[4,4,32,256]{3,0,2,1:T(4,128)}, f32[4,32,256]{2,1,0:T(8,128)})) %all-reduce.27.cloned.1.call-update) | async-done | bytes 655376 | tf_op jit(solution)/shard_map/psum | solution.py:122
  416.6 5.9 fusion.127
  422.5 40.4 %psum.158 = f32[4]{0:T(128)S(1)} all-reduce(f32[4]{0:T(128)} %get-tuple-element.107), channel_id=1, replica_groups=mesh['slab'=16,'grp'=8] {'slab'}, use_global_device_ids=true, to_apply=%region_26.27 | all-reduce | flops 4 | bytes 32 | tf_op jit(solution)/shard_map/psum | solution.py:92
  463.6 3.1 subtract_reduce_fusion.2
  466.7 2.5 convolution_bitcast_fusion.2
  469.2 2.0 fusion.84
  475.9 3.5 collective-permute-done.22
  479.4 1.7 select_maximum_fusion.4
  481.2 51.0 %all-reduce.25.cloned.1.call-done = (f32[4,4,32,256]{3,0,2,1:T(4,128)}, f32[4,32,256]{2,1,0:T(8,128)}) async-done(((f32[4,4,32,256]{3,0,2,1:T(4,128)}, f32[4,32,256]{2,1,0:T(8,128)}), (f32[4,4,32,256]{3,0,2,1:T(4,128)}, f32[4,32,256]{2,1,0:T(8,128)})) %all-reduce.25.cloned.1.call-update) | async-done | bytes 655376 | tf_op jit(solution)/shard_map/psum | solution.py:122
  532.2 5.7 fusion.128
  537.9 40.4 %psum.161 = f32[4]{0:T(128)S(1)} all-reduce(f32[4]{0:T(128)} %get-tuple-element.109), channel_id=1, replica_groups=mesh['slab'=16,'grp'=8] {'slab'}, use_global_device_ids=true, to_apply=%region_31.32 | all-reduce | flops 4 | bytes 32 | tf_op jit(solution)/shard_map/psum | solution.py:92
  579.0 3.0 subtract_reduce_fusion.1
  582.0 2.5 convolution_bitcast_fusion.1
  584.5 2.0 fusion.81
  590.4 4.4 collective-permute-done.24
  594.7 1.7 select_maximum_fusion.2
  596.5 51.0 %all-reduce.23.cloned.1.call-done = (f32[4,4,32,256]{3,0,2,1:T(4,128)}, f32[4,32,256]{2,1,0:T(8,128)}) async-done(((f32[4,4,32,256]{3,0,2,1:T(4,128)}, f32[4,32,256]{2,1,0:T(8,128)}), (f32[4,4,32,256]{3,0,2,1:T(4,128)}, f32[4,32,256]{2,1,0:T(8,128)})) %all-reduce.23.cloned.1.call-update) | async-done | bytes 655376 | tf_op jit(solution)/shard_map/psum | solution.py:122
  647.6 5.9 fusion.129
  653.4 40.6 %psum.164 = f32[4]{0:T(128)S(1)} all-reduce(f32[4]{0:T(128)} %get-tuple-element.111), channel_id=1, replica_groups=mesh['slab'=16,'grp'=8] {'slab'}, use_global_device_ids=true, to_apply=%region_36.37 | all-reduce | flops 4 | bytes 32 | tf_op jit(solution)/shard_map/psum | solution.py:92
  694.7 3.0 subtract_reduce_fusion
  697.7 2.5 convolution_bitcast_fusion
  700.5 2.1 fusion.78
  702.6 62.4 %psum.167 = f32[4,4]{1,0:T(4,128)S(1)} all-reduce(f32[4,4]{1,0:T(4,128)S(1)} %convolution_add_fusion), channel_id=1, replica_groups=mesh['slab'=16,'grp'=8] {'slab','grp'}, use_global_device_ids=true, to_apply=%region_40.41 | all-reduce | flops 16 | bytes 128 | tf_op jit(solution)/shard_map/psum | solution.py:163
  768.9 4.4 collective-permute-done.26
  773.9 56.6 %all-reduce.21.cloned.1.call-done = (f32[4,4,32,256]{3,0,2,1:T(4,128)}, f32[4,32,256]{2,1,0:T(8,128)}) async-done(((f32[4,4,32,256]{3,0,2,1:T(4,128)}, f32[4,32,256]{2,1,0:T(8,128)}), (f32[4,4,32,256]{3,0,2,1:T(4,128)}, f32[4,32,256]{2,1,0:T(8,128)})) %all-reduce.21.cloned.1.call-update) | async-done | bytes 655376 | tf_op jit(solution)/shard_map/psum | solution.py:122
  830.5 3.0 fusion.20
  (211 shorter events, 50.1 us)
Async XLA Ops:
  7.2 23.4 %copy-start = (f32[4,4]{1,0:T(4,128)S(1)}, f32[4,4]{1,0:T(4,128)}, u32[]{:S(2)}) copy-start(f32[4,4]{1,0:T(4,128)} %param.9) | copy-start | bytes 196
  7.2 409.4 %all-reduce.27.cloned.1.call-start = ((), (), s32[]{:S(2)}) async-start(), calls=%async_computation.3 | async-start | bytes 1310720 | tf_op jit(solution)/shard_map/psum | solution.py:122
  9.4 2.0 collective-permute-start
  11.5 14.3 %collective-permute-start.1 = (f32[4,4,32,256]{3,0,2,1:T(4,128)S(1)}, f32[4,4,32,256]{3,0,2,1:T(4,128)S(1)}, u32[]{:S(2)}, u32[]{:S(2)}) collective-permute-start(f32[4,4,32,256]{3,0,2,1:T(4,128)S(1)} %add.415), channel_id=1, source_target_pairs={{0,2},{1,3},{2,0},{3,1},{4,6},{5,7},{6,4},{7,5},{8,10},{9,11},{10,... | collective-permute-start | bytes 1572872 | tf_op jit(solution)/shard_map/ppermute | solution.py:48
  14.0 15.8 %copy-start.42 = (s32[4,32,256]{2,1,0:T(8,128)S(1)}, s32[4,32,256]{2,1,0:T(8,128)}, u32[]{:S(2)}) copy-start(s32[4,32,256]{2,1,0:T(8,128)} %param.7) | copy-start | bytes 393220
  14.0 16.8 %collective-permute-start.4 = (f32[4,1,32,256]{3,0,2,1:T(4,128)S(1)}, f32[4,1,32,256]{3,0,2,1:T(4,128)S(1)}, u32[]{:S(2)}, u32[]{:S(2)}) collective-permute-start(f32[4,1,32,256]{3,0,2,1:T(4,128)S(1)} %get-tuple-element.79), channel_id=1, source_target_pairs={{0,8},{8,16},{16,24},{24,32},{32,40},{40,48},{48,56},{56,64},{64,7... | collective-permute-start | bytes 393224 | tf_op jit(solution)/shard_map/ppermute | solution.py:20
  17.5 13.1 %copy-start.43 = (s32[4]{0:T(128)S(1)}, s32[4]{0:T(128)}, u32[]{:S(2)}) copy-start(s32[4]{0:T(128)} %param.8) | copy-start | bytes 52
  17.6 13.3 %collective-permute-start.3 = (f32[4,1,32,256]{3,0,2,1:T(4,128)S(1)}, f32[4,1,32,256]{3,0,2,1:T(4,128)S(1)}, u32[]{:S(2)}, u32[]{:S(2)}) collective-permute-start(f32[4,1,32,256]{3,0,2,1:T(4,128)S(1)} %get-tuple-element.80), channel_id=1, source_target_pairs={{8,0},{16,8},{24,16},{32,24},{40,32},{48,40},{56,48},{64,56},{72,6... | collective-permute-start | bytes 393224 | tf_op jit(solution)/shard_map/ppermute | solution.py:22
  26.0 15.1 %collective-permute-start.2 = (f32[4,4,32,256]{3,0,2,1:T(4,128)S(1)}, f32[4,4,32,256]{3,0,2,1:T(4,128)S(1)}, u32[]{:S(2)}, u32[]{:S(2)}) collective-permute-start(f32[4,4,32,256]{3,0,2,1:T(4,128)S(1)} %add.416), channel_id=1, source_target_pairs={{0,4},{1,5},{2,6},{3,7},{4,0},{5,1},{6,2},{7,3},{8,12},{9,13},{10,... | collective-permute-start | bytes 1572872 | tf_op jit(solution)/shard_map/ppermute | solution.py:48
  30.6 54.3 %copy-start.22 = (f32[4,32,256]{2,1,0:T(8,128)}, f32[4,32,256]{2,1,0:T(8,128)S(1)}, u32[]{:S(2)}) copy-start(f32[4,32,256]{2,1,0:T(8,128)S(1)} %convert_element_type.22) | copy-start | bytes 393220
  44.2 40.7 %copy-start.4 = (f32[4,4,32,256]{3,0,2,1:T(4,128)}, f32[4,4,32,256]{3,0,2,1:T(4,128)S(1)}, u32[]{:S(2)}) copy-start(f32[4,4,32,256]{3,0,2,1:T(4,128)S(1)} %get-tuple-element.62) | copy-start | bytes 1572868
  44.2 42.2 %copy-start.6 = (f32[4,4,32,256]{3,0,2,1:T(4,128)}, f32[4,4,32,256]{3,0,2,1:T(4,128)S(1)}, u32[]{:S(2)}) copy-start(f32[4,4,32,256]{3,0,2,1:T(4,128)S(1)} %get-tuple-element.103) | copy-start | bytes 1572868
  86.5 2.0 collective-permute-start.5
  88.6 14.0 %collective-permute-start.6 = (f32[4,4,32,256]{3,0,2,1:T(4,128)S(1)}, f32[4,4,32,256]{3,0,2,1:T(4,128)S(1)}, u32[]{:S(2)}, u32[]{:S(2)}) collective-permute-start(f32[4,4,32,256]{3,0,2,1:T(4,128)S(1)} %add.426), channel_id=1, source_target_pairs={{0,2},{1,3},{2,0},{3,1},{4,6},{5,7},{6,4},{7,5},{8,10},{9,11},{10,... | collective-permute-start | bytes 1572872 | tf_op jit(solution)/shard_map/ppermute | solution.py:48
  102.8 14.7 %collective-permute-start.7 = (f32[4,4,32,256]{3,0,2,1:T(4,128)S(1)}, f32[4,4,32,256]{3,0,2,1:T(4,128)S(1)}, u32[]{:S(2)}, u32[]{:S(2)}) collective-permute-start(f32[4,4,32,256]{3,0,2,1:T(4,128)S(1)} %add.427), channel_id=1, source_target_pairs={{0,4},{1,5},{2,6},{3,7},{4,0},{5,1},{6,2},{7,3},{8,12},{9,13},{10,... | collective-permute-start | bytes 1572872 | tf_op jit(solution)/shard_map/ppermute | solution.py:48
  106.1 3.8 collective-permute-start.9
  107.4 6.9 collective-permute-start.8
  108.7 47.5 %copy-start.24 = (f32[4,32,256]{2,1,0:T(8,128)}, f32[4,32,256]{2,1,0:T(8,128)S(1)}, u32[]{:S(2)}) copy-start(f32[4,32,256]{2,1,0:T(8,128)S(1)} %convert_element_type.23) | copy-start | bytes 393220
  120.6 36.9 %copy-start.10 = (f32[4,4,32,256]{3,0,2,1:T(4,128)}, f32[4,4,32,256]{3,0,2,1:T(4,128)S(1)}, u32[]{:S(2)}) copy-start(f32[4,4,32,256]{3,0,2,1:T(4,128)S(1)} %get-tuple-element.59) | copy-start | bytes 1572868
  120.6 36.9 %copy-start.12 = (f32[4,4,32,256]{3,0,2,1:T(4,128)}, f32[4,4,32,256]{3,0,2,1:T(4,128)S(1)}, u32[]{:S(2)}) copy-start(f32[4,4,32,256]{3,0,2,1:T(4,128)S(1)} %get-tuple-element.104) | copy-start | bytes 1572868
  157.5 2.0 collective-permute-start.10
  159.6 14.0 %collective-permute-start.11 = (f32[4,4,32,256]{3,0,2,1:T(4,128)S(1)}, f32[4,4,32,256]{3,0,2,1:T(4,128)S(1)}, u32[]{:S(2)}, u32[]{:S(2)}) collective-permute-start(f32[4,4,32,256]{3,0,2,1:T(4,128)S(1)} %add.437), channel_id=1, source_target_pairs={{0,2},{1,3},{2,0},{3,1},{4,6},{5,7},{6,4},{7,5},{8,10},{9,11},{10,... | collective-permute-start | bytes 1572872 | tf_op jit(solution)/shard_map/ppermute | solution.py:48
  173.8 14.8 %collective-permute-start.12 = (f32[4,4,32,256]{3,0,2,1:T(4,128)S(1)}, f32[4,4,32,256]{3,0,2,1:T(4,128)S(1)}, u32[]{:S(2)}, u32[]{:S(2)}) collective-permute-start(f32[4,4,32,256]{3,0,2,1:T(4,128)S(1)} %add.438), channel_id=1, source_target_pairs={{0,4},{1,5},{2,6},{3,7},{4,0},{5,1},{6,2},{7,3},{8,12},{9,13},{10,... | collective-permute-start | bytes 1572872 | tf_op jit(solution)/shard_map/ppermute | solution.py:48
  177.2 6.4 collective-permute-start.14
  181.1 6.9 collective-permute-start.13
  192.2 40.1 %copy-start.16 = (f32[4,4,32,256]{3,0,2,1:T(4,128)}, f32[4,4,32,256]{3,0,2,1:T(4,128)S(1)}, u32[]{:S(2)}) copy-start(f32[4,4,32,256]{3,0,2,1:T(4,128)S(1)} %get-tuple-element.56) | copy-start | bytes 1572868
  192.2 40.1 %copy-start.18 = (f32[4,4,32,256]{3,0,2,1:T(4,128)}, f32[4,4,32,256]{3,0,2,1:T(4,128)S(1)}, u32[]{:S(2)}) copy-start(f32[4,4,32,256]{3,0,2,1:T(4,128)S(1)} %get-tuple-element.105) | copy-start | bytes 1572868
  232.4 2.0 collective-permute-start.15
  234.5 20.8 %copy-start.41 = (pred[4,32,256]{2,1,0:T(8,128)(4,1)S(1)}, pred[4,32,256]{2,1,0:T(8,128)(4,1)}, u32[]{:S(2)}) copy-start(pred[4,32,256]{2,1,0:T(8,128)(4,1)} %get-tuple-element.52) | copy-start | bytes 98308
  234.5 14.0 %collective-permute-start.16 = (f32[4,4,32,256]{3,0,2,1:T(4,128)S(1)}, f32[4,4,32,256]{3,0,2,1:T(4,128)S(1)}, u32[]{:S(2)}, u32[]{:S(2)}) collective-permute-start(f32[4,4,32,256]{3,0,2,1:T(4,128)S(1)} %add.448), channel_id=1, source_target_pairs={{0,2},{1,3},{2,0},{3,1},{4,6},{5,7},{6,4},{7,5},{8,10},{9,11},{10,... | collective-permute-start | bytes 1572872 | tf_op jit(solution)/shard_map/ppermute | solution.py:48
  248.7 14.7 %collective-permute-start.17 = (f32[4,4,32,256]{3,0,2,1:T(4,128)S(1)}, f32[4,4,32,256]{3,0,2,1:T(4,128)S(1)}, u32[]{:S(2)}, u32[]{:S(2)}) collective-permute-start(f32[4,4,32,256]{3,0,2,1:T(4,128)S(1)} %add.449), channel_id=1, source_target_pairs={{0,4},{1,5},{2,6},{3,7},{4,0},{5,1},{6,2},{7,3},{8,12},{9,13},{10,... | collective-permute-start | bytes 1572872 | tf_op jit(solution)/shard_map/ppermute | solution.py:48
  252.1 4.4 collective-permute-start.19
  254.0 6.9 collective-permute-start.18
  263.9 39.1 %copy-start.26 = (f32[4,32,256]{2,1,0:T(8,128)S(1)}, f32[4,32,256]{2,1,0:T(8,128)}, u32[]{:S(2)}) copy-start(f32[4,32,256]{2,1,0:T(8,128)} %get-tuple-element.51) | copy-start | bytes 393220
  351.6 5.1 collective-permute-start.21
  353.6 6.9 collective-permute-start.20
  355.9 176.3 %all-reduce.25.cloned.1.call-start = ((), (), s32[]{:S(2)}) async-start(), calls=%async_computation.2 | async-start | bytes 1310720 | tf_op jit(solution)/shard_map/psum | solution.py:122
  356.8 59.8 %copy-start.37 = (f32[4,1,32,256]{3,0,2,1:T(4,128)}, f32[4,1,32,256]{3,0,2,1:T(4,128)S(1)}, u32[]{:S(2)}) copy-start(f32[4,1,32,256]{3,0,2,1:T(4,128)S(1)} %collective-permute-done.21) | copy-start | bytes 393220
  360.5 56.1 %copy-start.39 = (f32[4,1,32,256]{3,0,2,1:T(4,128)}, f32[4,1,32,256]{3,0,2,1:T(4,128)S(1)}, u32[]{:S(2)}) copy-start(f32[4,1,32,256]{3,0,2,1:T(4,128)S(1)} %collective-permute-done.20) | copy-start | bytes 393220
  416.6 47.0 %copy-start.17 = (f32[4,4,32,256]{3,0,2,1:T(4,128)S(1)}, f32[4,4,32,256]{3,0,2,1:T(4,128)}, u32[]{:S(2)}) copy-start(f32[4,4,32,256]{3,0,2,1:T(4,128)} %copy-done.16) | copy-start | bytes 1572868
  416.6 47.0 %copy-start.49 = (f32[4]{0:T(128)S(1)}, f32[4]{0:T(128)}, u32[]{:S(2)}) copy-start(f32[4]{0:T(128)} %copy-done.48) | copy-start | bytes 52
  471.3 4.6 collective-permute-start.23
  472.6 6.9 collective-permute-start.22
  473.9 58.3 %copy-start.13 = (f32[4,4,32,256]{3,0,2,1:T(4,128)S(1)}, f32[4,4,32,256]{3,0,2,1:T(4,128)}, u32[]{:S(2)}) copy-start(f32[4,4,32,256]{3,0,2,1:T(4,128)} %copy-done.12) | copy-start | bytes 1572868
  473.9 58.3 %copy-start.29 = (f32[4,32,256]{2,1,0:T(8,128)S(1)}, f32[4,32,256]{2,1,0:T(8,128)}, u32[]{:S(2)}) copy-start(f32[4,32,256]{2,1,0:T(8,128)} %get-tuple-element.89) | copy-start | bytes 393220
  473.9 173.6 %all-reduce.23.cloned.1.call-start = ((), (), s32[]{:S(2)}) async-start(), calls=%async_computation.1 | async-start | bytes 1310720 | tf_op jit(solution)/shard_map/psum | solution.py:122
  475.9 56.3 %copy-start.38 = (f32[4,1,32,256]{3,0,2,1:T(4,128)}, f32[4,1,32,256]{3,0,2,1:T(4,128)S(1)}, u32[]{:S(2)}) copy-start(f32[4,1,32,256]{3,0,2,1:T(4,128)S(1)} %collective-permute-done.23) | copy-start | bytes 393220
  479.4 52.7 %copy-start.40 = (f32[4,1,32,256]{3,0,2,1:T(4,128)}, f32[4,1,32,256]{3,0,2,1:T(4,128)S(1)}, u32[]{:S(2)}) copy-start(f32[4,1,32,256]{3,0,2,1:T(4,128)S(1)} %collective-permute-done.22) | copy-start | bytes 393220
  532.2 46.8 %copy-start.11 = (f32[4,4,32,256]{3,0,2,1:T(4,128)S(1)}, f32[4,4,32,256]{3,0,2,1:T(4,128)}, u32[]{:S(2)}) copy-start(f32[4,4,32,256]{3,0,2,1:T(4,128)} %copy-done.10) | copy-start | bytes 1572868
  532.2 46.8 %copy-start.47 = (f32[4]{0:T(128)S(1)}, f32[4]{0:T(128)}, u32[]{:S(2)}) copy-start(f32[4]{0:T(128)} %copy-done.46) | copy-start | bytes 52
  586.6 3.8 collective-permute-start.25
  587.9 6.9 collective-permute-start.24
  589.2 58.3 %copy-start.7 = (f32[4,4,32,256]{3,0,2,1:T(4,128)S(1)}, f32[4,4,32,256]{3,0,2,1:T(4,128)}, u32[]{:S(2)}) copy-start(f32[4,4,32,256]{3,0,2,1:T(4,128)} %copy-done.6) | copy-start | bytes 1572868
  589.2 58.3 %copy-start.28 = (f32[4,32,256]{2,1,0:T(8,128)S(1)}, f32[4,32,256]{2,1,0:T(8,128)}, u32[]{:S(2)}) copy-start(f32[4,32,256]{2,1,0:T(8,128)} %get-tuple-element.91) | copy-start | bytes 393220
  589.2 58.3 %copy-start.34 = (f32[4,32,256]{2,1,0:T(8,128)S(1)}, f32[4,32,256]{2,1,0:T(8,128)}, u32[]{:S(2)}) copy-start(f32[4,32,256]{2,1,0:T(8,128)} %copy-done.33) | copy-start | bytes 393220
  589.2 241.3 %all-reduce.21.cloned.1.call-start = ((), (), s32[]{:S(2)}) async-start(), calls=%async_computation | async-start | bytes 1310720 | tf_op jit(solution)/shard_map/psum | solution.py:122
  647.5 47.2 %copy-start.5 = (f32[4,4,32,256]{3,0,2,1:T(4,128)S(1)}, f32[4,4,32,256]{3,0,2,1:T(4,128)}, u32[]{:S(2)}) copy-start(f32[4,4,32,256]{3,0,2,1:T(4,128)} %copy-done.4) | copy-start | bytes 1572868
  647.5 47.2 %copy-start.23 = (f32[4,32,256]{2,1,0:T(8,128)S(1)}, f32[4,32,256]{2,1,0:T(8,128)}, u32[]{:S(2)}) copy-start(f32[4,32,256]{2,1,0:T(8,128)} %copy-done.22) | copy-start | bytes 393220
  647.5 47.2 %copy-start.27 = (f32[4,32,256]{2,1,0:T(8,128)S(1)}, f32[4,32,256]{2,1,0:T(8,128)}, u32[]{:S(2)}) copy-start(f32[4,32,256]{2,1,0:T(8,128)} %get-tuple-element.81) | copy-start | bytes 393220
  647.5 47.2 %copy-start.45 = (f32[4]{0:T(128)S(1)}, f32[4]{0:T(128)}, u32[]{:S(2)}) copy-start(f32[4]{0:T(128)} %copy-done.44) | copy-start | bytes 52
  765.0 3.9 collective-permute-start.27
  766.3 7.0 collective-permute-start.26
  767.6 62.9 %copy-start.30 = (f32[4,4,32,256]{3,0,2,1:T(4,128)S(1)}, f32[4,4,32,256]{3,0,2,1:T(4,128)}, u32[]{:S(2)}) copy-start(f32[4,4,32,256]{3,0,2,1:T(4,128)} %get-tuple-element.112) | copy-start | bytes 1572868
  767.6 62.9 %copy-start.32 = (f32[4,32,256]{2,1,0:T(8,128)S(1)}, f32[4,32,256]{2,1,0:T(8,128)}, u32[]{:S(2)}) copy-start(f32[4,32,256]{2,1,0:T(8,128)} %copy-done.31) | copy-start | bytes 393220
  (26 other events, 80.2 us)
Sparse Core Ops, SparseCore 0:
  356.0 60.5 all-reduce.26
  474.0 58.0 all-reduce.24
  589.3 58.1 all-reduce.22
  767.8 62.6 all-reduce.20
